TPU v7x, 32 devices: a whole 2x2x4 slice. The times are simulated.
32 devices in a mesh: groups: 2 (over x), tensor: 16 (over z, y, core).
Axes of the slice: x: 2, y: 2, z: 4, core: 2. Of those that a mesh axis runs over, the one named last changes fastest.
Arguments:
- image_features: bfloat16 [256, 12800], P('groups', 'tensor'), parts along dimension 0, may hold values from -6 to 6
- image_counts: int32 [4], P('groups'), parts along dimension 0, may hold values from 1 to 64, 80 in all
- slot_position: int32 [256], P('groups'), parts along dimension 0, may hold values from 0 to 255, as said below
- text_ids: int32 [512], P('groups'), parts along dimension 0, may hold values from 0 to 49151
- norm_gain: float32 [12800], replicated, may hold values from 0.5 to 1.5
- norm_bias: float32 [12800], replicated, may hold values from -3 to 3
- proj_first: bfloat16 [6144, 12800], P('tensor'), may hold values from -0.0546875 to 0.0546875
- proj_second: bfloat16 [6144, 6144], P('tensor'), may hold values from -0.078125 to 0.078125
- embedding: bfloat16 [6144, 49152], P('tensor'), may hold values from -6 to 6
- rms_gain: float32 [6144], replicated, may hold values from 0.5 to 1.5
- gate_weight: bfloat16 [6144, 16384], P(None, 'tensor'), may hold values from -0.109375 to 0.109375
- up_weight: bfloat16 [6144, 16384], P(None, 'tensor'), may hold values from -0.109375 to 0.109375
- down_weight: bfloat16 [16384, 6144], P('tensor'), may hold values from -0.046875 to 0.046875
- output_grad: bfloat16 [512, 6144], P('groups', 'tensor'), parts along dimension 0, may hold values from -6 to 6
Outputs:
- input_grad: float32 [512, 6144], P('groups', 'tensor'), parts along dimension 0
- second_grad: float32 [12288, 6144], P(('groups', 'tensor')), parts along dimension 0
There are 2 independent parts, one for each index of `groups`. A program takes and returns all parts, laid end to end along the dimension named above; an argument that names none is the same for every part. Nothing has to cross between parts.
Inputs may be any that keep to these rules, and one draw needn't show every extreme that they name: `image_counts`: the counts sum to 80. `slot_position`: the 128 positions are distinct.
All inputs are finite; a program needn't handle non-finite values.
Results may differ from a plain program's by a relative error of at most 0.0079.
Values may be sent and summed in bfloat16 or wider, within the bound.
No kernel may reach another device: no remote copies, remote signals or barrier semaphores. Data moves between devices by JAX's collectives and lax.ppermute only.
A program may use at most 192 MiB of HBM per device.

v0:
```python
import jax
import jax.numpy as jnp
from jax import lax
from jax.sharding import PartitionSpec as P

LIVE = 80


def layer_norm(rows_in, gain_in, bias_in):
    values = rows_in.astype(jnp.float32)
    centre = values - jnp.mean(values, axis=-1, keepdims=True)
    spread = jnp.mean(centre * centre, axis=-1, keepdims=True)
    return (centre * lax.rsqrt(spread + 1e-05) * gain_in + bias_in).astype(jnp.bfloat16)


def on_device(
    image_features,
    image_counts,
    slot_position,
    text_ids,
    norm_gain,
    norm_bias,
    proj_first,
    proj_second,
    embedding,
    rms_gain,
    gate_weight,
    up_weight,
    down_weight,
    output_grad,
):
    slot_total = image_features.shape[0]
    per_image = slot_total // image_counts.shape[0]
    seq_len = output_grad.shape[0]
    model_width = gate_weight.shape[0]
    col_count = output_grad.shape[1]
    slot_ids = jnp.arange(slot_total, dtype=jnp.int32)
    is_live = slot_ids % per_image < jnp.repeat(
        image_counts, per_image, total_repeat_length=slot_total
    )
    packed_order = jnp.argsort(jnp.where(is_live, 0, 1).astype(jnp.int32), stable=True)[:LIVE]
    gathered = lax.all_gather(image_features[packed_order], "tensor", axis=1, tiled=True)
    positions = slot_position[packed_order]
    in_use = jnp.ones((LIVE,), dtype=bool)
    normed = layer_norm(gathered, norm_gain, norm_bias)
    hidden_pre = lax.dot_general(
        normed, proj_first, (((1,), (1,)), ((), ())), preferred_element_type=jnp.float32
    )
    act_cols = jax.nn.gelu(hidden_pre, approximate=False).astype(jnp.bfloat16)
    act_full = lax.all_gather(act_cols, "tensor", axis=1, tiled=True)
    projected = lax.dot_general(
        act_full, proj_second, (((1,), (1,)), ((), ())), preferred_element_type=jnp.float32
    ).astype(jnp.bfloat16)
    target = jnp.where(in_use, positions, seq_len)
    text_rows = jnp.take(embedding, text_ids, axis=1).T
    tokens = text_rows.at[target].set(projected, mode="drop")
    full_tokens = lax.all_gather(tokens, "tensor", axis=1, tiled=True)
    values = full_tokens.astype(jnp.float32)
    inverse = lax.rsqrt(jnp.mean(values * values, axis=-1, keepdims=True) + 1e-05)
    normed_tokens = (values * inverse * rms_gain).astype(jnp.bfloat16)
    gate_out = jnp.dot(normed_tokens, gate_weight, preferred_element_type=jnp.float32)
    up_out = jnp.dot(normed_tokens, up_weight, preferred_element_type=jnp.float32)
    hidden_grad = lax.dot_general(
        lax.all_gather(output_grad, "tensor", axis=1, tiled=True),
        down_weight,
        (((1,), (1,)), ((), ())),
        preferred_element_type=jnp.float32,
    )
    sig_gate = jax.nn.sigmoid(gate_out)
    gate_grad = (hidden_grad * up_out * sig_gate * (1.0 + gate_out * (1.0 - sig_gate))).astype(
        jnp.bfloat16
    )
    up_grad = (hidden_grad * gate_out * sig_gate).astype(jnp.bfloat16)
    partial_value = lax.dot_general(
        gate_grad, gate_weight, (((1,), (1,)), ((), ())), preferred_element_type=jnp.float32
    )
    partial_value = partial_value + lax.dot_general(
        up_grad, up_weight, (((1,), (1,)), ((), ())), preferred_element_type=jnp.float32
    )
    norm_grad = lax.psum_scatter(partial_value, "tensor", scatter_dimension=1, tiled=True)
    offset = lax.axis_index("tensor") * col_count
    gain_cols = lax.dynamic_slice_in_dim(rms_gain, offset, col_count, 0)
    unit_cols = tokens.astype(jnp.float32) * inverse
    scaled = gain_cols * norm_grad
    row_sums = lax.psum(jnp.sum(scaled * unit_cols, axis=-1), "tensor")
    input_grad = output_grad.astype(jnp.float32) + inverse * (
        scaled - unit_cols * (row_sums / model_width)[:, None]
    )
    proj_grad = jnp.where(in_use[:, None], input_grad[positions], 0.0).astype(jnp.bfloat16)
    second_grad = lax.dot_general(
        proj_grad, act_full, (((0,), (0,)), ((), ())), preferred_element_type=jnp.float32
    )
    return (input_grad, second_grad)


def solution(mesh):
    placed = (
        P("groups", "tensor"),
        P("groups"),
        P("groups"),
        P("groups"),
        P(),
        P(),
        P("tensor", None),
        P("tensor", None),
        P("tensor", None),
        P(),
        P(None, "tensor"),
        P(None, "tensor"),
        P("tensor", None),
        P("groups", "tensor"),
    )
    return jax.shard_map(
        on_device,
        mesh=mesh,
        in_specs=placed,
        out_specs=(P("groups", "tensor"), P(("groups", "tensor"), None)),
        check_vma=False,
    )
```

profile of v0, /device:TPU:0, one launch (start us, length us, event | category | flops | bytes accessed | tf_op | source)
XLA Modules:
  0.0 335.2 jit_solution(3321569869737275003)
XLA Ops:
  7.2 0.0 copy-start
  7.2 0.0 all-gather.10.cloned.1.call-start
  7.2 1.3 fusion.38
  8.5 2.0 compare_select_fusion.3
  10.5 2.5 sort.17
  13.0 1.1 copy.22
  14.1 1.4 gather_fusion.2
  15.5 0.0 all-gather.10.cloned.1.call-update
  15.6 0.0 all-gather.8.cloned.1.call-start
  15.6 0.7 all-gather.8.cloned.1.call-update
  16.3 0.0 copy-start.8
  16.3 0.0 all-gather.6.cloned.1.call-start
  16.4 46.7 %copy.21 = bf16[384,49152]{0,1:T(8,128)(2,1)} copy(bf16[384,49152]{1,0:T(8,128)(2,1)} %param.24) | data formatting | bytes 75497472 | tf_op args[8]
  63.1 1.2 gather_fusion.1
  64.3 2.8 gather_fusion
  67.1 0.1 broadcast_select_fusion
  67.2 0.0 all-gather.10.cloned.1.call-done
  67.3 0.0 copy-start.3
  67.3 4.4 %copy.23 = f32[16,800,80]{1,0,2:T(8,128)} copy(bf16[16,800,80]{1,2,0:T(8,128)(2,1)} %all-gather.10.cloned.1.call-done) | data formatting | bytes 6144000 | tf_op jit(solution)/shard_map/convert_element_type | solution.py:10
  71.7 5.9 %reshape.138 = f32[12800,80]{0,1:T(8,128)} reshape(f32[16,800,80]{1,0,2:T(8,128)} %copy.23) | data formatting | bytes 8192000 | tf_op jit(solution)/shard_map/convert_element_type | solution.py:10
  77.6 0.4 convert_reduce_fusion
  78.0 2.9 multiply_reduce_fusion
  81.0 0.0 slice-start.1
  81.0 7.5 %fusion.23 = bf16[80,384]{1,0:T(8,128)(2,1)S(1)} fusion(bf16[384,12800]{1,0:T(8,128)(2,1)} %param.22, f32[12800,80]{0,1:T(8,128)S(1)} %copy-done.2, f32[12800]{0:T(1024)S(1)} %copy-done.10, f32[80]{0:T(128)S(1)} %add_rsqrt_fusion.1, f32[80]{0:T(128)S(1)} %broadcast_multiply_fusion.1, f32[12800]{0:T(1024)S(1)} %copy-done.11), kind=kOutput, calls=%fused_computation.38 | convolution fusion | flops 793548800 | bytes 14090880 | tf_op jit(solution)/shard_map/dot_general | solution.py:46
  88.5 29.3 %all_gather.13 = bf16[80,6144]{1,0:T(8,128)(2,1)S(1)} all-gather(bf16[80,384]{1,0:T(8,128)(2,1)S(1)} %fusion.23), channel_id=1, replica_groups=mesh['groups'=2,'tensor'=16] {'tensor'}, dimensions={1}, use_global_device_ids=true | all-gather | bytes 1044480 | tf_op jit(solution)/shard_map/all_gather | solution.py:50
  117.8 1.5 convolution_convert_fusion
  119.3 1.0 scatter_fusion
  120.4 0.0 copy-start.4
  120.4 0.7 copy-done.4
  121.0 0.0 all-gather.6.cloned.1.call-update
  121.1 0.0 copy-start.9
  121.1 0.2 reduce-scatter.2.cloned.1.call-start
  121.3 0.0 all-gather.8.cloned.1.call-done
  121.3 7.5 %fusion.39 = f32[256,1024]{1,0:T(8,128)S(1)} fusion(bf16[256,6144]{1,0:T(8,128)(2,1)} %all-gather.8.cloned.1.call-done, bf16[1024,6144]{1,0:T(8,128)(2,1)} %param.28), kind=kOutput, calls=%fused_computation.73 | convolution fusion | flops 3221225472 | bytes 16777216 | tf_op jit(solution)/shard_map/dot_general | solution.py:63
  128.8 35.8 %all-gather.6.cloned.1.call-done = bf16[256,6144]{1,0:T(8,128)(2,1)} async-done(((bf16[256,384]{1,0:T(8,128)(2,1)}), bf16[256,6144]{1,0:T(8,128)(2,1)}) %all-gather.6.cloned.1.call-update) | async-done | bytes 3145744 | tf_op jit(solution)/shard_map/all_gather | solution.py:57
  164.7 2.6 fusion
  167.3 10.0 %fusion.13 = f32[256,1024]{1,0:T(8,128)} fusion(bf16[6144,1024]{1,0:T(8,128)(2,1)} %param.26, bf16[256,6144]{1,0:T(8,128)(2,1)} %all-gather.6.cloned.1.call-done, f32[6144]{0:T(1024)S(1)} %copy-done.9, f32[256]{0:T(256)S(1)} %add_rsqrt_fusion), kind=kOutput, calls=%fused_computation.27 | convolution fusion | flops 3227516928 | bytes 16802816 | tf_op jit(solution)/shard_map/dot_general | solution.py:61
  177.3 16.0 %fusion.17 = f32[256,6144]{1,0:T(8,128)} fusion(bf16[6144,1024]{1,0:T(8,128)(2,1)} %param.26, f32[256,1024]{1,0:T(8,128)S(1)} %fusion.39, bf16[6144,1024]{1,0:T(8,128)(2,1)} %param.27, f32[256,1024]{1,0:T(8,128)} %fusion.13, bf16[256,6144]{1,0:T(8,128)(2,1)} %all-gather.6.cloned.1.call-done, f32[6144]{0:T(1024)S(1)} %copy-done.9, f32[256]{0:T(256)S(1)} %add_rsqrt_fusion), kind=kOutput, calls=%fused_computation.28 | convolution fusion | flops 6451363840 | bytes 36725760 | tf_op jit(solution)/shard_map/dot_general | solution.py:74
  193.3 12.9 %convolution_add_fusion = f32[256,6144]{1,0:T(8,128)} fusion(f32[256,6144]{1,0:T(8,128)} %fusion.17, bf16[6144,1024]{1,0:T(8,128)(2,1)} %param.27, f32[256,1024]{1,0:T(8,128)S(1)} %fusion.39, f32[256,1024]{1,0:T(8,128)} %fusion.13), kind=kOutput, calls=%fused_computation.7 | convolution fusion | flops 3224371200 | bytes 27262976 | tf_op jit(solution)/shard_map/dot_general | solution.py:77
  206.2 0.0 reduce-scatter.2.cloned.1.call-update
  206.2 0.1 dynamic_slice.3
  206.3 83.2 %reduce-scatter.2.cloned.1.call-done = f32[256,384]{1,0:T(8,128)} async-done(((f32[256,6144]{1,0:T(8,128)}), f32[256,384]{1,0:T(8,128)}) %reduce-scatter.2.cloned.1.call-update) | async-done | bytes 393232 | tf_op jit(solution)/shard_map/reduce_scatter | solution.py:80
  289.5 1.2 multiply_reduce_fusion.1
  290.7 30.8 %psum.7 = f32[256]{0:T(256)S(1)} all-reduce(f32[256]{0:T(256)S(1)} %multiply_reduce_fusion.1), channel_id=1, replica_groups=mesh['groups'=2,'tensor'=16] {'tensor'}, use_global_device_ids=true, to_apply=%region_7.8 | all-reduce | flops 256 | bytes 2048 | tf_op jit(solution)/shard_map/psum | solution.py:85
  321.6 1.2 multiply_add_fusion
  322.8 0.0 copy-start.6
  322.8 0.7 gather_fusion.3
  323.5 5.2 %fusion.40 = f32[384,6144]{1,0:T(8,128)} fusion(bf16[80,384]{1,0:T(8,128)(2,1)S(1)} %gather_fusion.3, bf16[80,6144]{1,0:T(8,128)(2,1)S(1)} %all_gather.13), kind=kOutput, calls=%fused_computation.74 | convolution fusion | flops 377487360 | bytes 10481664 | tf_op jit(solution)/shard_map/dot_general | solution.py:90
  (33 shorter events, 0.1 us)
Async XLA Ops:
  7.2 55.9 %copy-start = (s32[128]{0:T(128)S(1)}, s32[128]{0:T(128)}, u32[]{:S(2)}) copy-start(s32[128]{0:T(128)} %param.18) | copy-start | bytes 1540
  7.2 60.1 %all-gather.10.cloned.1.call-start = ((), (), s32[]{:S(2)}) async-start(), calls=%async_computation.4 | async-start | bytes 2437120 | tf_op jit(solution)/shard_map/all_gather | solution.py:42
  15.6 105.8 %all-gather.8.cloned.1.call-start = ((), (), s32[]{:S(2)}) async-start(), calls=%async_computation.2 | async-start | bytes 3342336 | tf_op jit(solution)/shard_map/all_gather | solution.py:64
  16.3 48.0 %copy-start.8 = (s32[256]{0:T(256)S(1)}, s32[256]{0:T(256)}, u32[]{:S(2)}) copy-start(s32[256]{0:T(256)} %param.19) | copy-start | bytes 3076
  16.3 148.3 %all-gather.6.cloned.1.call-start = ((), (), s32[]{:S(2)}) async-start(), calls=%async_computation.1 | async-start | bytes 3342336 | tf_op jit(solution)/shard_map/all_gather | solution.py:57
  67.3 10.3 %copy-start.3 = (bf16[16,800,80]{1,2,0:T(8,128)(2,1)S(1)}, bf16[16,800,80]{1,2,0:T(8,128)(2,1)}, u32[]{:S(2)}) copy-start(bf16[16,800,80]{1,2,0:T(8,128)(2,1)} %all-gather.10.cloned.1.call-done) | copy-start | bytes 6144004
  71.7 9.3 %copy-start.10 = (f32[12800]{0:T(1024)S(1)}, f32[12800]{0:T(1024)}, u32[]{:S(2)}) copy-start(f32[12800]{0:T(1024)} %param.20) | copy-start | bytes 153604
  71.7 9.3 %copy-start.11 = (f32[12800]{0:T(1024)S(1)}, f32[12800]{0:T(1024)}, u32[]{:S(2)}) copy-start(f32[12800]{0:T(1024)} %param.21) | copy-start | bytes 153604
  77.6 3.4 %copy-start.2 = (f32[12800,80]{0,1:T(8,128)S(1)}, f32[12800,80]{0,1:T(8,128)}, u32[]{:S(2)}) copy-start(f32[12800,80]{0,1:T(8,128)} %reshape.138) | copy-start | bytes 12288004
  78.0 39.8 %slice-start = ((s8[4718592]{0:T(1024)(128)(4,1)}), s8[4194304]{0:T(1024)(128)(4,1)S(1)}, s32[]{:S(2)}) async-start(s8[4718592]{0:T(1024)(128)(4,1)} %bitcast.29), calls=%async_computation.5 | async-start | bytes 8388608
  81.0 36.8 %slice-start.1 = ((s8[4718592]{0:T(1024)(128)(4,1)}), s8[524288]{0:T(1024)(128)(4,1)S(1)}, s32[]{:S(2)}) async-start(s8[4718592]{0:T(1024)(128)(4,1)} %bitcast.29), calls=%async_computation.6 | async-start | bytes 1048576
  120.4 0.7 copy-start.4
  121.1 46.2 %copy-start.9 = (f32[6144]{0:T(1024)S(1)}, f32[6144]{0:T(1024)}, u32[]{:S(2)}) copy-start(f32[6144]{0:T(1024)} %param.25) | copy-start | bytes 73732
  121.1 168.5 %reduce-scatter.2.cloned.1.call-start = ((), (), s32[]{:S(2)}) async-start(), calls=%async_computation.3 | async-start | bytes 6684672 | tf_op jit(solution)/shard_map/reduce_scatter | solution.py:80
  206.2 83.4 %copy-start.5 = (bf16[256,384]{1,0:T(8,128)(2,1)S(1)}, bf16[256,384]{1,0:T(8,128)(2,1)}, u32[]{:S(2)}) copy-start(bf16[256,384]{1,0:T(8,128)(2,1)} %copy-done.4) | copy-start | bytes 589828
  206.2 115.4 %copy-start.7 = (bf16[256,384]{1,0:T(8,128)(2,1)S(1)}, bf16[256,384]{1,0:T(8,128)(2,1)}, u32[]{:S(2)}) copy-start(bf16[256,384]{1,0:T(8,128)(2,1)} %param.29) | copy-start | bytes 589828
  206.3 122.3 %copy-start.1 = (s32[128]{0:T(128)S(1)}, s32[128]{0:T(128)}, u32[]{:S(2)}) copy-start(s32[128]{0:T(128)} %param.18) | copy-start | bytes 1540
  322.8 5.9 %copy-start.6 = (f32[256,384]{1,0:T(8,128)}, f32[256,384]{1,0:T(8,128)S(1)}, u32[]{:S(2)}) copy-start(f32[256,384]{1,0:T(8,128)S(1)} %multiply_add_fusion) | copy-start | bytes 1179652
Sparse Core Ops, SparseCore 0:
  15.7 45.1 all-gather.9
  63.0 48.9 all-gather.7
  121.2 43.4 all-gather.5
  206.3 83.1 reduce-scatter.1
where the time goes:
time: 337 us; the launch traced here: 335 us
  waiting for transfers between devices  120 us (36%)
  local copies, waits for them, and re-layouts  67.3 us (20%)
  matrix products  60.5 us (18%)
  blocking collectives  60.1 us (18%)
  between operations  14 us (4%)
  other arithmetic  13 us (4%)
    reduce_scatter x1, waiting for transfers between devices, on_device(): lax.psum_scatter(partial_value, 'tensor', scatter_dimension=1, tiled=True)  83.2 us
    unnamed x30, local copies, waits for them, and re-layouts  48.5 us
    all_gather x1, waiting for transfers between devices, on_device(): full_tokens = lax.all_gather(tokens, 'tensor', axis=1, tiled=True)  35.8 us
    psum x1, blocking collectives, on_device(): row_sums = lax.psum(jnp.sum(scaled * unit_cols, axis=-1), 'tensor')  30.8 us
    all_gather x1, blocking collectives, on_device(): act_full = lax.all_gather(act_cols, 'tensor', axis=1, tiled=True)  29.3 us
    dot_general x1, matrix products, on_device(): lax.dot_general(gate_grad, gate_weight, (((1,), (1,)), ((), ())), preferr...  16 us
    dot_general x1, matrix products, on_device(): lax.dot_general(up_grad, up_weight, (((1,), (1,)), ((), ())), preferred_e...  12.9 us
    convert_element_type x2, local copies, waits for them, and re-layouts, layer_norm(): values = rows_in.astype(jnp.float32)  10.3 us
  transfers between devices with their start and end apart: 4, of which 2 were waited for; matrix products, arithmetic and copies ran while one was open for 24% of the time, Pallas kernels for 0%

commit v1 on v0

--- a/solution.py
+++ b/solution.py
@@ -82,7 +82,9 @@
     gain_cols = lax.dynamic_slice_in_dim(rms_gain, offset, col_count, 0)
     unit_cols = tokens.astype(jnp.float32) * inverse
     scaled = gain_cols * norm_grad
-    row_sums = lax.psum(jnp.sum(scaled * unit_cols, axis=-1), "tensor")
+    block = jnp.sum(scaled * unit_cols, axis=-1)
+    parts = lax.all_gather(block, "tensor")
+    row_sums = jnp.sum(parts, axis=0)
     input_grad = output_grad.astype(jnp.float32) + inverse * (
         scaled - unit_cols * (row_sums / model_width)[:, None]
     )

time: 337 us -> 326 us (0.967)
  blocking collectives: 60.1 us -> 48.9 us
    psum x1 -> x0, blocking collectives: 30.8 us -> none  [on_device(): row_sums = lax.psum(jnp.sum(scaled * unit_cols, axis=-1), 'tensor')]
    all_gather x0 -> x1, blocking collectives: none -> 19.6 us  [on_device(): parts = lax.all_gather(block, 'tensor')]
  transfers between devices with their start and end apart: 4 -> 4, of which waited for: 2 -> 2; matrix products, arithmetic and copies ran while one was open for 24% -> 25% of each run, Pallas kernels for 0% -> 0%
where the time goes in v1:
time: 326 us; the launch traced here: 324 us
  waiting for transfers between devices  120 us (37%)
  local copies, waits for them, and re-layouts  67.3 us (21%)
  matrix products  60.5 us (19%)
  blocking collectives  48.9 us (15%)
  between operations  14 us (4%)
  other arithmetic  13 us (4%)
    reduce_scatter x1, waiting for transfers between devices, on_device(): lax.psum_scatter(partial_value, 'tensor', scatter_dimension=1, tiled=True)  83.2 us
    unnamed x30, local copies, waits for them, and re-layouts  48.5 us
    all_gather x1, waiting for transfers between devices, on_device(): full_tokens = lax.all_gather(tokens, 'tensor', axis=1, tiled=True)  35.8 us
    all_gather x1, blocking collectives, on_device(): act_full = lax.all_gather(act_cols, 'tensor', axis=1, tiled=True)  29.3 us
    all_gather x1, blocking collectives, on_device(): parts = lax.all_gather(block, 'tensor')  19.6 us
    dot_general x1, matrix products, on_device(): lax.dot_general(gate_grad, gate_weight, (((1,), (1,)), ((), ())), preferr...  16 us
    dot_general x1, matrix products, on_device(): lax.dot_general(up_grad, up_weight, (((1,), (1,)), ((), ())), preferred_e...  12.9 us
    convert_element_type x2, local copies, waits for them, and re-layouts, layer_norm(): values = rows_in.astype(jnp.float32)  10.3 us
  transfers between devices with their start and end apart: 4, of which 2 were waited for; matrix products, arithmetic and copies ran while one was open for 25% of the time, Pallas kernels for 0%

profile of v1, /device:TPU:0, one launch (start us, length us, event | category | flops | bytes accessed | tf_op | source)
XLA Modules:
  0.0 324.0 jit_solution(12364418901481566084)
XLA Ops:
  7.2 0.0 copy-start
  7.2 0.0 all-gather.12.cloned.1.call-start
  7.2 1.3 fusion.38
  8.5 2.0 compare_select_fusion.3
  10.5 2.5 sort.17
  13.0 1.1 copy.22
  14.1 1.4 gather_fusion.2
  15.5 0.0 all-gather.12.cloned.1.call-update
  15.6 0.0 all-gather.10.cloned.1.call-start
  15.6 0.7 all-gather.10.cloned.1.call-update
  16.3 0.0 copy-start.8
  16.3 0.0 all-gather.8.cloned.1.call-start
  16.4 46.7 %copy.21 = bf16[384,49152]{0,1:T(8,128)(2,1)} copy(bf16[384,49152]{1,0:T(8,128)(2,1)} %param.24) | data formatting | bytes 75497472 | tf_op args[8]
  63.1 1.2 gather_fusion.1
  64.3 2.8 gather_fusion
  67.1 0.1 broadcast_select_fusion
  67.2 0.0 all-gather.12.cloned.1.call-done
  67.3 0.0 copy-start.3
  67.3 4.4 %copy.23 = f32[16,800,80]{1,0,2:T(8,128)} copy(bf16[16,800,80]{1,2,0:T(8,128)(2,1)} %all-gather.12.cloned.1.call-done) | data formatting | bytes 6144000 | tf_op jit(solution)/shard_map/convert_element_type | solution.py:10
  71.7 5.9 %reshape.144 = f32[12800,80]{0,1:T(8,128)} reshape(f32[16,800,80]{1,0,2:T(8,128)} %copy.23) | data formatting | bytes 8192000 | tf_op jit(solution)/shard_map/convert_element_type | solution.py:10
  77.6 0.4 convert_reduce_fusion
  78.0 2.9 multiply_reduce_fusion
  81.0 0.0 slice-start.1
  81.0 7.5 %fusion.23 = bf16[80,384]{1,0:T(8,128)(2,1)S(1)} fusion(bf16[384,12800]{1,0:T(8,128)(2,1)} %param.22, f32[12800,80]{0,1:T(8,128)S(1)} %copy-done.2, f32[12800]{0:T(1024)S(1)} %copy-done.10, f32[80]{0:T(128)S(1)} %add_rsqrt_fusion.1, f32[80]{0:T(128)S(1)} %broadcast_multiply_fusion.1, f32[12800]{0:T(1024)S(1)} %copy-done.11), kind=kOutput, calls=%fused_computation.38 | convolution fusion | flops 793548800 | bytes 14090880 | tf_op jit(solution)/shard_map/dot_general | solution.py:46
  88.5 29.3 %all_gather.19 = bf16[80,6144]{1,0:T(8,128)(2,1)S(1)} all-gather(bf16[80,384]{1,0:T(8,128)(2,1)S(1)} %fusion.23), channel_id=1, replica_groups=mesh['groups'=2,'tensor'=16] {'tensor'}, dimensions={1}, use_global_device_ids=true | all-gather | bytes 1044480 | tf_op jit(solution)/shard_map/all_gather | solution.py:50
  117.8 1.5 convolution_convert_fusion
  119.3 1.0 scatter_fusion
  120.4 0.0 copy-start.4
  120.4 0.7 copy-done.4
  121.0 0.0 all-gather.8.cloned.1.call-update
  121.1 0.0 copy-start.9
  121.1 0.2 reduce-scatter.2.cloned.1.call-start
  121.3 0.0 all-gather.10.cloned.1.call-done
  121.3 7.5 %fusion.39 = f32[256,1024]{1,0:T(8,128)S(1)} fusion(bf16[256,6144]{1,0:T(8,128)(2,1)} %all-gather.10.cloned.1.call-done, bf16[1024,6144]{1,0:T(8,128)(2,1)} %param.28), kind=kOutput, calls=%fused_computation.73 | convolution fusion | flops 3221225472 | bytes 16777216 | tf_op jit(solution)/shard_map/dot_general | solution.py:63
  128.8 35.8 %all-gather.8.cloned.1.call-done = bf16[256,6144]{1,0:T(8,128)(2,1)} async-done(((bf16[256,384]{1,0:T(8,128)(2,1)}), bf16[256,6144]{1,0:T(8,128)(2,1)}) %all-gather.8.cloned.1.call-update) | async-done | bytes 3145744 | tf_op jit(solution)/shard_map/all_gather | solution.py:57
  164.7 2.6 fusion
  167.3 10.0 %fusion.13 = f32[256,1024]{1,0:T(8,128)} fusion(bf16[6144,1024]{1,0:T(8,128)(2,1)} %param.26, bf16[256,6144]{1,0:T(8,128)(2,1)} %all-gather.8.cloned.1.call-done, f32[6144]{0:T(1024)S(1)} %copy-done.9, f32[256]{0:T(256)S(1)} %add_rsqrt_fusion), kind=kOutput, calls=%fused_computation.27 | convolution fusion | flops 3227516928 | bytes 16802816 | tf_op jit(solution)/shard_map/dot_general | solution.py:61
  177.3 16.0 %fusion.17 = f32[256,6144]{1,0:T(8,128)} fusion(bf16[6144,1024]{1,0:T(8,128)(2,1)} %param.26, f32[256,1024]{1,0:T(8,128)S(1)} %fusion.39, bf16[6144,1024]{1,0:T(8,128)(2,1)} %param.27, f32[256,1024]{1,0:T(8,128)} %fusion.13, bf16[256,6144]{1,0:T(8,128)(2,1)} %all-gather.8.cloned.1.call-done, f32[6144]{0:T(1024)S(1)} %copy-done.9, f32[256]{0:T(256)S(1)} %add_rsqrt_fusion), kind=kOutput, calls=%fused_computation.28 | convolution fusion | flops 6451363840 | bytes 36725760 | tf_op jit(solution)/shard_map/dot_general | solution.py:74
  193.3 12.9 %convolution_add_fusion = f32[256,6144]{1,0:T(8,128)} fusion(f32[256,6144]{1,0:T(8,128)} %fusion.17, bf16[6144,1024]{1,0:T(8,128)(2,1)} %param.27, f32[256,1024]{1,0:T(8,128)S(1)} %fusion.39, f32[256,1024]{1,0:T(8,128)} %fusion.13), kind=kOutput, calls=%fused_computation.7 | convolution fusion | flops 3224371200 | bytes 27262976 | tf_op jit(solution)/shard_map/dot_general | solution.py:77
  206.2 0.0 reduce-scatter.2.cloned.1.call-update
  206.2 0.1 dynamic_slice.3
  206.3 83.2 %reduce-scatter.2.cloned.1.call-done = f32[256,384]{1,0:T(8,128)} async-done(((f32[256,6144]{1,0:T(8,128)}), f32[256,384]{1,0:T(8,128)}) %reduce-scatter.2.cloned.1.call-update) | async-done | bytes 393232 | tf_op jit(solution)/shard_map/reduce_scatter | solution.py:80
  289.5 1.2 multiply_reduce_fusion.1
  290.7 19.6 %all-gather.3 = f32[16,1,256]{2,1,0:T(1,128)S(1)} all-gather(f32[1,1,256]{2,1,0:T(1,128)S(1)} %bitcast.33), channel_id=3, replica_groups=mesh['groups'=2,'tensor'=16] {'tensor'}, dimensions={0}, use_global_device_ids=true | all-gather | bytes 17408 | tf_op jit(solution)/shard_map/all_gather | solution.py:86
  310.4 1.2 multiply_add_fusion
  311.6 0.0 copy-start.6
  311.6 0.7 gather_fusion.3
  312.3 5.2 %fusion.40 = f32[384,6144]{1,0:T(8,128)} fusion(bf16[80,384]{1,0:T(8,128)(2,1)S(1)} %gather_fusion.3, bf16[80,6144]{1,0:T(8,128)(2,1)S(1)} %all_gather.19), kind=kOutput, calls=%fused_computation.74 | convolution fusion | flops 377487360 | bytes 10481664 | tf_op jit(solution)/shard_map/dot_general | solution.py:92
  (34 shorter events, 0.1 us)
Async XLA Ops:
  7.2 55.9 %copy-start = (s32[128]{0:T(128)S(1)}, s32[128]{0:T(128)}, u32[]{:S(2)}) copy-start(s32[128]{0:T(128)} %param.18) | copy-start | bytes 1540
  7.2 60.1 %all-gather.12.cloned.1.call-start = ((), (), s32[]{:S(2)}) async-start(), calls=%async_computation.4 | async-start | bytes 2437120 | tf_op jit(solution)/shard_map/all_gather | solution.py:42
  15.6 105.8 %all-gather.10.cloned.1.call-start = ((), (), s32[]{:S(2)}) async-start(), calls=%async_computation.2 | async-start | bytes 3342336 | tf_op jit(solution)/shard_map/all_gather | solution.py:64
  16.3 48.0 %copy-start.8 = (s32[256]{0:T(256)S(1)}, s32[256]{0:T(256)}, u32[]{:S(2)}) copy-start(s32[256]{0:T(256)} %param.19) | copy-start | bytes 3076
  16.3 148.3 %all-gather.8.cloned.1.call-start = ((), (), s32[]{:S(2)}) async-start(), calls=%async_computation.1 | async-start | bytes 3342336 | tf_op jit(solution)/shard_map/all_gather | solution.py:57
  67.3 10.3 %copy-start.3 = (bf16[16,800,80]{1,2,0:T(8,128)(2,1)S(1)}, bf16[16,800,80]{1,2,0:T(8,128)(2,1)}, u32[]{:S(2)}) copy-start(bf16[16,800,80]{1,2,0:T(8,128)(2,1)} %all-gather.12.cloned.1.call-done) | copy-start | bytes 6144004
  71.7 9.3 %copy-start.10 = (f32[12800]{0:T(1024)S(1)}, f32[12800]{0:T(1024)}, u32[]{:S(2)}) copy-start(f32[12800]{0:T(1024)} %param.20) | copy-start | bytes 153604
  71.7 9.3 %copy-start.11 = (f32[12800]{0:T(1024)S(1)}, f32[12800]{0:T(1024)}, u32[]{:S(2)}) copy-start(f32[12800]{0:T(1024)} %param.21) | copy-start | bytes 153604
  77.6 3.4 %copy-start.2 = (f32[12800,80]{0,1:T(8,128)S(1)}, f32[12800,80]{0,1:T(8,128)}, u32[]{:S(2)}) copy-start(f32[12800,80]{0,1:T(8,128)} %reshape.144) | copy-start | bytes 12288004
  78.0 39.8 %slice-start = ((s8[4718592]{0:T(1024)(128)(4,1)}), s8[4194304]{0:T(1024)(128)(4,1)S(1)}, s32[]{:S(2)}) async-start(s8[4718592]{0:T(1024)(128)(4,1)} %bitcast.30), calls=%async_computation.5 | async-start | bytes 8388608
  81.0 36.8 %slice-start.1 = ((s8[4718592]{0:T(1024)(128)(4,1)}), s8[524288]{0:T(1024)(128)(4,1)S(1)}, s32[]{:S(2)}) async-start(s8[4718592]{0:T(1024)(128)(4,1)} %bitcast.30), calls=%async_computation.6 | async-start | bytes 1048576
  120.4 0.7 copy-start.4
  121.1 46.2 %copy-start.9 = (f32[6144]{0:T(1024)S(1)}, f32[6144]{0:T(1024)}, u32[]{:S(2)}) copy-start(f32[6144]{0:T(1024)} %param.25) | copy-start | bytes 73732
  121.1 168.5 %reduce-scatter.2.cloned.1.call-start = ((), (), s32[]{:S(2)}) async-start(), calls=%async_computation.3 | async-start | bytes 6684672 | tf_op jit(solution)/shard_map/reduce_scatter | solution.py:80
  206.2 83.4 %copy-start.5 = (bf16[256,384]{1,0:T(8,128)(2,1)S(1)}, bf16[256,384]{1,0:T(8,128)(2,1)}, u32[]{:S(2)}) copy-start(bf16[256,384]{1,0:T(8,128)(2,1)} %copy-done.4) | copy-start | bytes 589828
  206.2 104.2 %copy-start.7 = (bf16[256,384]{1,0:T(8,128)(2,1)S(1)}, bf16[256,384]{1,0:T(8,128)(2,1)}, u32[]{:S(2)}) copy-start(bf16[256,384]{1,0:T(8,128)(2,1)} %param.29) | copy-start | bytes 589828
  206.3 111.2 %copy-start.1 = (s32[128]{0:T(128)S(1)}, s32[128]{0:T(128)}, u32[]{:S(2)}) copy-start(s32[128]{0:T(128)} %param.18) | copy-start | bytes 1540
  311.6 5.9 %copy-start.6 = (f32[256,384]{1,0:T(8,128)}, f32[256,384]{1,0:T(8,128)S(1)}, u32[]{:S(2)}) copy-start(f32[256,384]{1,0:T(8,128)S(1)} %multiply_add_fusion) | copy-start | bytes 1179652
Sparse Core Ops, SparseCore 0:
  15.7 45.1 all-gather.11
  63.0 48.9 all-gather.9
  121.2 43.4 all-gather.7
  206.3 83.1 reduce-scatter.1
